TPU v7x, 32 devices: a whole 2x2x4 slice. The times are simulated.
32 devices in a mesh: seq: 2 (over y), dp: 16 (over z, x, core).
Axes of the slice: x: 2, y: 2, z: 4, core: 2. Of those that a mesh axis runs over, the one named last changes fastest.
Arguments:
- tokens: bfloat16 [16, 512, 1024], P('dp', 'seq'), may hold values from -6 to 6
- starts: int32 [16, 512], P('dp', 'seq'), may hold values 0 or 1
- routes: int32 [16, 512, 8], P('dp', 'seq'), may hold values from 0 to 15, all different within a row; in each aligned block of 256 rows (0 to 255, 256 to 511, ..., all dimensions but the last counted through in order) at most 224 rows name the same one
- gain_one: bfloat16 [1024], P('dp'), may hold values from 0.5 to 1.5
- query_key_value_weight: bfloat16 [1024, 2048], P('dp'), may hold values from -0.1875 to 0.1875
- w_out: bfloat16 [1024, 1024], P('dp'), may hold values from -1.5 to 1.5
- gain_two: bfloat16 [1024], P('dp'), may hold values from 0.5 to 1.5
- w_router: bfloat16 [1024, 16], P('dp'), may hold values from -0.09375 to 0.09375
- w_gate_up: bfloat16 [1024, 16, 1024], P('dp'), may hold values from -0.1875 to 0.1875
- w_down: bfloat16 [512, 16, 1024], P('dp'), may hold values from -1 to 1
- cotangent: bfloat16 [16, 512, 1024], P('dp', 'seq'), may hold values from -6 to 6
Outputs:
- output: bfloat16 [16, 512, 1024], P('dp', 'seq')
- input_grad: bfloat16 [16, 512, 1024], P('dp', 'seq')
- grad_gain_one: float32 [1024], P('dp')
- grad_w_qkv: float32 [1024, 2048], P('dp')
- grad_w_out: float32 [1024, 1024], P('dp')
- grad_gain_two: float32 [1024], P('dp')
- grad_w_router: float32 [1024, 16], P('dp')
- grad_w_gate_up: float32 [1024, 16, 1024], P('dp')
- grad_w_down: float32 [512, 16, 1024], P('dp')
- stream_rms: float32 [16, 2], P('dp')
Inputs may be any that keep to these rules, and one draw needn't show every extreme that they name: `starts`: 1 marks a token that begins a document; a stream's first token begins one whatever its entry. `routes`: each row names 8 different experts; within the 256 rows of one device no expert is named more than 224 times, and in every draw some expert is named exactly 224 times on some device.
All inputs are finite; a program needn't handle non-finite values. No bound on the sum of `starts` on one device may be relied on, other than what follows from the above.
Results may differ from a plain program's by a relative error of at most 0.015.
Values may be sent and summed in bfloat16 or wider, within the bound.
A program may use at most 384 MiB of HBM per device.

v0:
```python
import jax
import jax.numpy as jnp
from jax import lax
from jax.sharding import PartitionSpec as P

MODEL_WIDTH = 1024
QUERY_HEADS = 16
KEY_VALUE_HEADS = 8
HEAD_SIZE = 64
F = 512
EXPERTS = 16
TOPK = 8
CAP = 224
epsilon = 1e-06
rope_base = 10000.0
highest = lax.Precision.HIGHEST
masked_score = -1e30


def rms_normed(token_rows, gain_row):
    inverse = lax.rsqrt(jnp.mean(token_rows * token_rows, axis=-1, keepdims=True) + epsilon)
    return token_rows * inverse * gain_row


def norm_back(token_rows, gain_row, upstream):
    inverse = lax.rsqrt(jnp.mean(token_rows * token_rows, axis=-1, keepdims=True) + epsilon)
    gain_grad = jnp.sum(upstream * token_rows * inverse, axis=0)
    scaled = upstream * gain_row
    rows_grad = inverse * scaled - token_rows * inverse**3 * jnp.mean(
        scaled * token_rows, axis=-1, keepdims=True
    )
    return (rows_grad, gain_grad)


def rope_tables(positions, head_dim):
    half_dim = head_dim // 2
    frequency = rope_base ** (-(jnp.arange(half_dim, dtype=jnp.float32) * 2.0) / head_dim)
    angles = positions.astype(jnp.float32)[:, None] * frequency[None, :]
    cosine_table = jnp.cos(angles)
    sine_values = jnp.sin(angles)
    return (
        jnp.concatenate([cosine_table, cosine_table], 1),
        jnp.concatenate([sine_values, sine_values], 1),
    )


def rotary_apply(head_rows, cosine_table, sine_values):
    half_dim = head_rows.shape[-1] // 2
    turned = jnp.concatenate([-head_rows[..., half_dim:], head_rows[..., :half_dim]], -1)
    return head_rows * cosine_table[:, None, :] + turned * sine_values[:, None, :]


def unrotate(grad_rows, cosine_table, sine_values):
    half_dim = grad_rows.shape[-1] // 2
    scaled = grad_rows * sine_values[:, None, :]
    back_turn = jnp.concatenate([scaled[..., half_dim:], -scaled[..., :half_dim]], -1)
    return grad_rows * cosine_table[:, None, :] + back_turn


def slot_tables(route_rows):
    pair_count = route_rows.shape[0] * route_rows.shape[1]
    flat_routes = route_rows.reshape(-1)
    one_hot = (flat_routes[:, None] == jnp.arange(EXPERTS, dtype=jnp.int32)[None, :]).astype(
        jnp.int32
    )
    earlier = jnp.cumsum(one_hot, axis=0) - one_hot
    within = jnp.sum(earlier * one_hot, axis=1)
    slot_flat = flat_routes * CAP + within
    pair_of_slot = (
        jnp.full((EXPERTS * CAP,), pair_count, jnp.int32)
        .at[slot_flat]
        .set(jnp.arange(pair_count, dtype=jnp.int32))
    )
    return (slot_flat.reshape(route_rows.shape), pair_of_slot)


def swiglu_parts(gate_up):
    gate_part = gate_up[..., :F]
    up_part = gate_up[..., F:]
    sigmoid_gate = jax.nn.sigmoid(gate_part)
    silu_gate = gate_part * sigmoid_gate
    act_low = (silu_gate * up_part).astype(jnp.bfloat16)
    return (gate_part, up_part, sigmoid_gate, silu_gate, act_low)


def swiglu_back(act_grad, gate_part, up_part, sigmoid_gate, silu_gate):
    gate_deriv = sigmoid_gate * (1.0 + gate_part * (1.0 - sigmoid_gate))
    return jnp.concatenate([act_grad * up_part * gate_deriv, act_grad * silu_gate], -1).astype(
        jnp.bfloat16
    )


def body(
    tokens,
    starts,
    routes,
    gain_one,
    query_key_value_weight,
    w_out,
    gain_two,
    w_router,
    w_gate_up,
    w_down,
    cotangent,
):
    token_count = tokens.shape[1]
    seq_rank = lax.axis_index("seq")
    token_rows = tokens[0].astype(jnp.float32)
    grad_output = cotangent[0].astype(jnp.float32)
    stream_flags = lax.all_gather(starts[0], "seq", axis=0, tiled=True)
    stream_index = jnp.arange(stream_flags.shape[0], dtype=jnp.int32)
    begins = jnp.where(stream_index == 0, 1, stream_flags)
    segment_all = jnp.cumsum(begins)
    last_begin = lax.cummax(jnp.where(begins > 0, stream_index, -1), axis=0)
    positions_all = stream_index - last_begin
    positions = lax.dynamic_slice_in_dim(positions_all, seq_rank * token_count, token_count)
    gain_one_all, qkv_weight, out_weight, gain_two_all, router_weight = (
        lax.all_gather(gain_one, "dp", axis=0, tiled=True),
        lax.all_gather(query_key_value_weight, "dp", axis=0, tiled=True),
        lax.all_gather(w_out, "dp", axis=0, tiled=True),
        lax.all_gather(gain_two, "dp", axis=0, tiled=True),
        lax.all_gather(w_router, "dp", axis=0, tiled=True),
    )
    gain_a = gain_one_all.astype(jnp.float32)
    gain_b = gain_two_all.astype(jnp.float32)
    query_columns = QUERY_HEADS * HEAD_SIZE
    key_value_columns = KEY_VALUE_HEADS * HEAD_SIZE
    normed_one = rms_normed(token_rows, gain_a).astype(jnp.bfloat16)
    projected_rows = jnp.dot(normed_one, qkv_weight, preferred_element_type=jnp.float32)
    cosine_table, sine_values = rope_tables(positions, HEAD_SIZE)
    queries_low = (
        rotary_apply(
            projected_rows[:, :query_columns].reshape(token_count, QUERY_HEADS, HEAD_SIZE),
            cosine_table,
            sine_values,
        )
        .reshape(token_count, query_columns)
        .astype(jnp.bfloat16)
    )
    keys_low = (
        rotary_apply(
            projected_rows[:, query_columns : query_columns + key_value_columns].reshape(
                token_count, KEY_VALUE_HEADS, HEAD_SIZE
            ),
            cosine_table,
            sine_values,
        )
        .reshape(token_count, key_value_columns)
        .astype(jnp.bfloat16)
    )
    values_low = projected_rows[:, query_columns + key_value_columns :].astype(jnp.bfloat16)
    query_heads, key_heads, value_heads = (
        lax.all_to_all(queries_low, "seq", split_axis=1, concat_axis=0, tiled=True),
        lax.all_to_all(keys_low, "seq", split_axis=1, concat_axis=0, tiled=True),
        lax.all_to_all(values_low, "seq", split_axis=1, concat_axis=0, tiled=True),
    )
    sequence_length = query_heads.shape[0]
    kv_local = key_heads.shape[1] // HEAD_SIZE
    query_group_width = QUERY_HEADS // KEY_VALUE_HEADS
    query_four = query_heads.reshape(sequence_length, kv_local, query_group_width, HEAD_SIZE)
    key_three = key_heads.reshape(sequence_length, kv_local, HEAD_SIZE)
    value_three = value_heads.reshape(sequence_length, kv_local, HEAD_SIZE)
    block_rows = min(512, sequence_length)
    score_scale = HEAD_SIZE ** (-0.5)
    key_index = jnp.arange(sequence_length, dtype=jnp.int32)

    def block_scores(row_start):
        scores = (
            jnp.einsum("qgrd,kgd->grqk", query_four, key_three, preferred_element_type=jnp.float32)
            * score_scale
        )
        query_index = row_start + jnp.arange(block_rows, dtype=jnp.int32)
        allowed = (segment_all[:, None] == segment_all[None, :]) & (
            key_index[None, :] <= query_index[:, None]
        )
        return (query_four, jnp.where(allowed[None, None], scores, masked_score))

    row_start = 0
    query_block, scores = block_scores(row_start)
    top_score = jnp.max(scores, axis=-1, keepdims=True)
    exp_scores = jnp.exp(scores - top_score)
    exp_total = jnp.sum(exp_scores, axis=-1, keepdims=True)
    probs_low = (exp_scores / exp_total).astype(jnp.bfloat16)
    block_out = jnp.einsum(
        "grqk,kgd->qgrd", probs_low, value_three, preferred_element_type=jnp.float32
    )
    outputs_list = block_out.reshape(block_rows, kv_local * query_group_width * HEAD_SIZE).astype(
        jnp.bfloat16
    )
    log_sums = [top_score + jnp.log(exp_total)]
    attended = lax.all_to_all(outputs_list, "seq", split_axis=0, concat_axis=1, tiled=True)
    hidden = token_rows + jnp.dot(attended, out_weight, preferred_element_type=jnp.float32)
    normed_two = rms_normed(hidden, gain_b).astype(jnp.bfloat16)
    logits = jnp.dot(normed_two, router_weight, preferred_element_type=jnp.float32)
    route_rows = routes[0]
    route_match = route_rows[:, :, None] == jnp.arange(EXPERTS, dtype=jnp.int32)[None, None, :]
    chosen = jnp.sum(jnp.where(route_match, logits[:, None, :], 0.0), axis=-1)
    gate_weights = jax.nn.softmax(chosen, axis=-1)
    slot_index, pair_of_slot = slot_tables(route_rows)
    token_of_slot = pair_of_slot // TOPK
    padded = jnp.concatenate([normed_two, jnp.zeros((1, MODEL_WIDTH), jnp.bfloat16)], 0)
    dispatched = padded[token_of_slot].reshape(EXPERTS, CAP, MODEL_WIDTH)
    pair_gate = jnp.concatenate([gate_weights.reshape(-1), jnp.zeros((1,), jnp.float32)])[
        pair_of_slot
    ]
    grad_padded = jnp.concatenate([grad_output, jnp.zeros((1, MODEL_WIDTH), jnp.float32)], 0)
    expert_grad = (
        (pair_gate[:, None] * grad_padded[token_of_slot])
        .astype(jnp.bfloat16)
        .reshape(EXPERTS, CAP, MODEL_WIDTH)
    )
    full_gate_up, full_down = (
        lax.all_gather(w_gate_up, "dp", axis=0, tiled=True),
        lax.all_gather(w_down, "dp", axis=0, tiled=True),
    )
    gate_up = jnp.einsum(
        "ecd,def->ecf", dispatched, full_gate_up, preferred_element_type=jnp.float32
    )
    gate_part, up_part, sigmoid_gate, silu_gate, act_low = swiglu_parts(gate_up)
    expert_out = jnp.einsum("ecf,fed->ecd", act_low, full_down, preferred_element_type=jnp.float32)
    act_grad = jnp.einsum(
        "ecd,fed->ecf", expert_grad, full_down, preferred_element_type=jnp.float32
    )
    down_wgrad = jnp.einsum(
        "ecf,ecd->fed", act_low, expert_grad, preferred_element_type=jnp.float32
    )
    gate_up_grad = swiglu_back(act_grad, gate_part, up_part, sigmoid_gate, silu_gate)
    gate_up_wgrad = jnp.einsum(
        "ecd,ecf->def", dispatched, gate_up_grad, preferred_element_type=jnp.float32
    )
    dispatched_grad = jnp.einsum(
        "ecf,def->ecd", gate_up_grad, full_gate_up, preferred_element_type=jnp.float32
    )
    expert_flat = expert_out.reshape(EXPERTS * CAP, MODEL_WIDTH)
    picked = expert_flat[slot_index]
    mixed = jnp.sum(gate_weights[:, :, None] * picked, axis=1)
    output = (hidden + mixed).astype(jnp.bfloat16)[None]
    stat_sums = jnp.stack([jnp.sum(hidden * hidden), jnp.sum(mixed * mixed)])
    gate_grad = jnp.sum(picked * grad_output[:, None, :], axis=-1)
    normed_grad = jnp.sum(dispatched_grad.reshape(EXPERTS * CAP, MODEL_WIDTH)[slot_index], axis=1)
    chosen_grad = gate_weights * (
        gate_grad - jnp.sum(gate_weights * gate_grad, axis=-1, keepdims=True)
    )
    logits_grad = jnp.sum(jnp.where(route_match, chosen_grad[:, :, None], 0.0), axis=1)
    router_float = router_weight.astype(jnp.float32)
    normed_grad = normed_grad + jnp.dot(logits_grad, router_float.T, precision=highest)
    router_wgrad = jnp.dot(normed_two.astype(jnp.float32).T, logits_grad, precision=highest)
    hidden_branch, gain_two_grad = norm_back(hidden, gain_b, normed_grad)
    hidden_grad = grad_output + hidden_branch
    branch_low = hidden_grad.astype(jnp.bfloat16)
    out_wgrad = jnp.einsum("tc,td->cd", attended, branch_low, preferred_element_type=jnp.float32)
    attended_grad = jnp.einsum(
        "td,cd->tc", branch_low, out_weight, preferred_element_type=jnp.float32
    ).astype(jnp.bfloat16)
    attended_grad_heads = lax.all_to_all(
        attended_grad, "seq", split_axis=1, concat_axis=0, tiled=True
    )
    row_start = 0
    query_block, scores = block_scores(row_start)
    probs = jnp.exp(scores - log_sums[row_start // block_rows])
    grad_block = attended_grad_heads.reshape(block_rows, kv_local, query_group_width, HEAD_SIZE)
    prob_grad = jnp.einsum(
        "qgrd,kgd->grqk", grad_block, value_three, preferred_element_type=jnp.float32
    )
    row_delta = jnp.sum(probs * prob_grad, axis=-1, keepdims=True)
    score_grad = (probs * (prob_grad - row_delta)).astype(jnp.bfloat16)
    block_query_grad = (
        jnp.einsum("grqk,kgd->qgrd", score_grad, key_three, preferred_element_type=jnp.float32)
        * score_scale
    )
    query_grads = block_query_grad.reshape(block_rows, kv_local * query_group_width * HEAD_SIZE)
    key_grad = (
        jnp.einsum("grqk,qgrd->kgd", score_grad, query_block, preferred_element_type=jnp.float32)
        * score_scale
    )
    value_grad = jnp.einsum(
        "grqk,qgrd->kgd", probs.astype(jnp.bfloat16), grad_block, preferred_element_type=jnp.float32
    )
    query_grad_low = query_grads.astype(jnp.bfloat16)
    key_grad_low = key_grad.reshape(sequence_length, kv_local * HEAD_SIZE).astype(jnp.bfloat16)
    value_grad_low = value_grad.reshape(sequence_length, kv_local * HEAD_SIZE).astype(jnp.bfloat16)
    query_grad_tok, key_grad_token_rows, value_grad_tok = (
        lax.all_to_all(query_grad_low, "seq", split_axis=0, concat_axis=1, tiled=True),
        lax.all_to_all(key_grad_low, "seq", split_axis=0, concat_axis=1, tiled=True),
        lax.all_to_all(value_grad_low, "seq", split_axis=0, concat_axis=1, tiled=True),
    )
    query_back = unrotate(
        query_grad_tok.astype(jnp.float32).reshape(token_count, QUERY_HEADS, HEAD_SIZE),
        cosine_table,
        sine_values,
    ).reshape(token_count, query_columns)
    key_back = unrotate(
        key_grad_token_rows.astype(jnp.float32).reshape(token_count, KEY_VALUE_HEADS, HEAD_SIZE),
        cosine_table,
        sine_values,
    ).reshape(token_count, key_value_columns)
    projected_grad = jnp.concatenate(
        [query_back, key_back, value_grad_tok.astype(jnp.float32)], 1
    ).astype(jnp.bfloat16)
    qkv_wgrad = jnp.einsum(
        "td,tc->dc", normed_one, projected_grad, preferred_element_type=jnp.float32
    )
    normed_one_grad = jnp.einsum(
        "tc,dc->td", projected_grad, qkv_weight, preferred_element_type=jnp.float32
    )
    rows_branch, gain_one_grad = norm_back(token_rows, gain_a, normed_one_grad)
    input_grad = (hidden_grad + rows_branch).astype(jnp.bfloat16)[None]
    (
        shard_gain_one,
        shard_qkv,
        shard_out,
        shard_gain_two,
        shard_router,
        shard_gate_up,
        shard_down,
    ) = (
        lax.psum_scatter(gain_one_grad, "dp", scatter_dimension=0, tiled=True),
        lax.psum_scatter(qkv_wgrad, "dp", scatter_dimension=0, tiled=True),
        lax.psum_scatter(out_wgrad, "dp", scatter_dimension=0, tiled=True),
        lax.psum_scatter(gain_two_grad, "dp", scatter_dimension=0, tiled=True),
        lax.psum_scatter(router_wgrad, "dp", scatter_dimension=0, tiled=True),
        lax.psum_scatter(gate_up_wgrad, "dp", scatter_dimension=0, tiled=True),
        lax.psum_scatter(down_wgrad, "dp", scatter_dimension=0, tiled=True),
    )
    summed = (
        lax.psum(shard_gain_one.astype(jnp.bfloat16), "seq").astype(jnp.float32),
        lax.psum(shard_qkv.astype(jnp.bfloat16), "seq").astype(jnp.float32),
        lax.psum(shard_out.astype(jnp.bfloat16), "seq").astype(jnp.float32),
        lax.psum(shard_gain_two.astype(jnp.bfloat16), "seq").astype(jnp.float32),
        lax.psum(shard_router.astype(jnp.bfloat16), "seq").astype(jnp.float32),
        lax.psum(shard_gate_up.astype(jnp.bfloat16), "seq").astype(jnp.float32),
        lax.psum(shard_down.astype(jnp.bfloat16), "seq").astype(jnp.float32),
        lax.psum(stat_sums.astype(jnp.bfloat16), "seq").astype(jnp.float32),
    )
    stream_rms = jnp.sqrt(summed[7] / (sequence_length * MODEL_WIDTH)).reshape(1, 2)
    return (
        output,
        input_grad,
        summed[0],
        summed[1],
        summed[2],
        summed[3],
        summed[4],
        summed[5],
        summed[6],
        stream_rms,
    )


def solution(mesh):
    placed = (
        P("dp", "seq", None),
        P("dp", "seq"),
        P("dp", "seq", None),
        P("dp"),
        P("dp", None),
        P("dp", None),
        P("dp"),
        P("dp", None),
        P("dp", None, None),
        P("dp", None, None),
        P("dp", "seq", None),
    )
    return jax.shard_map(
        body,
        mesh=mesh,
        in_specs=placed,
        out_specs=(
            P("dp", "seq", None),
            P("dp", "seq", None),
            P("dp"),
            P("dp", None),
            P("dp", None),
            P("dp"),
            P("dp", None),
            P("dp", None, None),
            P("dp", None, None),
            P("dp", None),
        ),
        check_vma=False,
    )
```

profile of v0, /device:TPU:0, one launch (start us, length us, event | category | flops | bytes accessed | tf_op | source)
XLA Modules:
  0.0 1841.7 jit_solution(11289706347054955673)
XLA Ops:
  16.7 35.8 %all-reduce.7 = (bf16[1024]{0:T(1024)(128)(2,1)S(1)}, bf16[1024]{0:T(1024)(128)(2,1)S(1)}) all-reduce(bf16[1024]{0:T(1024)(128)(2,1)S(1)} %dynamic-update-slice, bf16[1024]{0:T(1024)(128)(2,1)S(1)} %dynamic-update-slice.1), channel_id=1, replica_groups=mesh['seq'=2,'dp'=16] {'dp'}, use_global_device_ids=true, to_apply=%add.2 | all-reduce | flops 2048 | bytes 8192
  65.4 8.1 scatter_custom_fusion
  132.6 18.3 all-gather.1
  151.3 12.5 gather_fusion.3
  168.6 18.9 %gather_fusion.2 = f32[3584]{0:T(1024)S(1)} fusion(f32[2049]{0:T(1024)S(1)} %pad_maximum_fusion.10, s32[4096]{0:T(1024)S(1)} %get-tuple-element.83), kind=kCustom, calls=%fused_computation.2 | custom fusion | bytes 43008 | tf_op jit(solution)/shard_map/gather | solution.py:203
  187.6 11.9 gather_fusion
  199.6 75.6 %all-gather.11.cloned.1.call-done = bf16[1024,16,1024]{2,0,1:T(8,128)(2,1)} async-done(((bf16[64,16,1024]{2,0,1:T(8,128)(2,1)}), bf16[1024,16,1024]{2,0,1:T(8,128)(2,1)}) %all-gather.11.cloned.1.call-update) | async-done | bytes 33554448 | tf_op jit(solution)/shard_map/all_gather | solution.py:213
  275.1 23.0 %fusion.81 = f32[16,224,1024]{2,1,0:T(8,128)} fusion(bf16[16,224,1024]{2,1,0:T(8,128)(2,1)} %bitcast.243, bf16[1024,16,1024]{2,0,1:T(8,128)(2,1)} %all-gather.11.cloned.1.call-done), kind=kOutput, calls=%fused_computation.184 | convolution fusion | flops 7516192768 | bytes 55574528 | tf_op jit(solution)/shard_map/ecd,def->ecf/dot_general | solution.py:216
  298.1 105.8 %all-gather.13.cloned.1.call-done = bf16[512,16,1024]{2,0,1:T(8,128)(2,1)} async-done(((bf16[32,16,1024]{2,0,1:T(8,128)(2,1)}), bf16[512,16,1024]{2,0,1:T(8,128)(2,1)}) %all-gather.13.cloned.1.call-update) | async-done | bytes 16777232 | tf_op jit(solution)/shard_map/all_gather | solution.py:214
  404.0 24.3 %multiply_convert_fusion.2 = (bf16[16,224,512]{2,1,0:T(8,128)(2,1)}, bf16[16,224,512]{2,1,0:T(8,128)(2,1)}, bf16[16,224,512]{2,1,0:T(8,128)(2,1)}) fusion(f32[16,224,1024]{2,1,0:T(8,128)} %fusion.81, bf16[512,16,1024]{2,0,1:T(8,128)(2,1)} %all-gather.13.cloned.1.call-done, f32[16,224,1024]{2,1,0:T(8,128)} %bitcast.241, f32[16,224]{1,0:T(8,128)S(1)} %mul.376), kind=kOutput, calls=%fused_computation.26 | convolution fusion | flops 3792961536 | bytes 57161728 | tf_op jit(solution)/shard_map/ecd,fed->ecf/dot_general | solution.py:221
  428.3 21.6 %fusion.8 = f32[16,224,1024]{2,1,0:T(8,128)} fusion(bf16[1024,16,1024]{2,0,1:T(8,128)(2,1)} %all-gather.11.cloned.1.call-done, bf16[16,224,512]{2,1,0:T(8,128)(2,1)} %get-tuple-element.50, bf16[16,224,512]{2,1,0:T(8,128)(2,1)} %get-tuple-element.49), kind=kOutput, calls=%fused_computation.31 | convolution fusion | flops 7530872832 | bytes 55574528 | tf_op jit(solution)/shard_map/ecf,def->ecd/dot_general | solution.py:231
  449.9 17.1 gather_fusion.4
  473.5 13.5 fusion.82
  487.1 17.0 gather_fusion.1
  526.4 8.6 all-to-all-done.4
  586.3 20.1 %convolution_bitcast_fusion.1 = f32[512,16,1024]{0,2,1:T(8,128)} fusion(bf16[16,224,512]{2,1,0:T(8,128)(2,1)} %get-tuple-element.51, f32[16,224,1024]{2,1,0:T(8,128)} %bitcast.242, f32[16,224]{1,0:T(8,128)S(1)} %mul.376), kind=kOutput, calls=%fused_computation.8 | convolution fusion | flops 3765436416 | bytes 51918848 | tf_op jit(solution)/shard_map/ecf,ecd->fed/dot_general | solution.py:224
  606.4 34.0 %copy.163 = f32[512,16,1024]{2,1,0:T(8,128)} copy(f32[512,16,1024]{0,2,1:T(8,128)} %convolution_bitcast_fusion.1) | data formatting | bytes 67108864 | tf_op jit(solution)/shard_map/ecf,ecd->fed/transpose | solution.py:224
  640.6 29.2 %convolution_bitcast_fusion = f32[1024,16,1024]{0,2,1:T(8,128)} fusion(bf16[16,224,1024]{2,1,0:T(8,128)(2,1)} %bitcast.244, bf16[16,224,512]{2,1,0:T(8,128)(2,1)} %get-tuple-element.50, bf16[16,224,512]{2,1,0:T(8,128)(2,1)} %get-tuple-element.49), kind=kOutput, calls=%fused_computation.6 | convolution fusion | flops 7530872832 | bytes 81788928 | tf_op jit(solution)/shard_map/ecd,ecf->def/dot_general | solution.py:228
  669.7 68.0 %copy.162 = f32[1024,16,1024]{2,1,0:T(8,128)} copy(f32[1024,16,1024]{0,2,1:T(8,128)} %convolution_bitcast_fusion) | data formatting | bytes 134217728 | tf_op jit(solution)/shard_map/ecd,ecf->def/transpose | solution.py:228
  743.9 287.7 %reduce-scatter.14.cloned.1.call-done = f32[32,16,1024]{2,1,0:T(8,128)} async-done(((f32[512,16,1024]{2,1,0:T(8,128)}), f32[32,16,1024]{2,1,0:T(8,128)}) %reduce-scatter.14.cloned.1.call-update) | async-done | bytes 2097168 | tf_op jit(solution)/shard_map/reduce_scatter | solution.py:323
  1034.4 633.0 %reduce-scatter.12.cloned.1.call-done = f32[64,16,1024]{2,1,0:T(8,128)} async-done(((f32[1024,16,1024]{2,1,0:T(8,128)}), f32[64,16,1024]{2,1,0:T(8,128)}) %reduce-scatter.12.cloned.1.call-update) | async-done | bytes 4194320 | tf_op jit(solution)/shard_map/reduce_scatter | solution.py:322
  1673.4 53.5 %reduce-scatter.16.cloned.1.call-done = f32[64,16]{1,0:T(8,128)} async-done(((f32[1024,16]{1,0:T(8,128)}), f32[64,16]{1,0:T(8,128)}) %reduce-scatter.16.cloned.1.call-update) | async-done | bytes 4112
  1732.2 30.1 %all-reduce.6 = (bf16[1024]{0:T(1024)(128)(2,1)S(1)}, bf16[1024]{0:T(1024)(128)(2,1)S(1)}) all-reduce(f32[1024]{0:T(1024)S(1)} %get-tuple-element.34, f32[1024]{0:T(1024)S(1)} %copy-done.48), channel_id=3, replica_groups=mesh['seq'=2,'dp'=16] {'dp'}, use_global_device_ids=true, to_apply=%region_24.25.clone | all-reduce | flops 2048 | bytes 12288
  1772.2 51.8 %all-reduce.12.cloned.1.call-done = (bf16[64,2048]{1,0:T(8,128)(2,1)}, bf16[64,1024]{1,0:T(8,128)(2,1)}, bf16[64,16,1024]{2,1,0:T(8,128)(2,1)}, bf16[32,16,1024]{2,1,0:T(8,128)(2,1)}) async-done(((bf16[64,2048]{1,0:T(8,128)(2,1)}, bf16[64,1024]{1,0:T(8,128)(2,1)}, bf16[64,16,1024]{2,1,0:T(8,128)(2,1)}, bf16[32,16,1024]{2,1,0:T(8,128)(2,1)}), (bf16[64,2048]{1,0:T(8,128)(2,1)}, bf16[64,1024]{1,0:T(8,128)(2,1)}, ...) | async-done | bytes 3538960 | tf_op jit(solution)/shard_map/psum | solution.py:327
  (318 shorter events, 204.9 us)
Async XLA Ops:
  7.2 45.3 %copy-start.59 = (s32[1,256]{1,0:T(1,128)S(1)}, s32[1,256]{1,0:T(1,128)}, u32[]{:S(2)}) copy-start(s32[1,256]{1,0:T(1,128)} %param.12) | copy-start | bytes 3076
  7.2 68.2 %all-gather.7.cloned.1.call-start = ((), (), s32[]{:S(2)}) async-start(), calls=%async_computation.13 | async-start | bytes 4456448 | tf_op jit(solution)/shard_map/all_gather | solution.py:119
  8.0 155.8 %all-gather.9.cloned.1.call-start = ((), (), s32[]{:S(2)}) async-start(), calls=%async_computation.14 | async-start | bytes 2228224 | tf_op jit(solution)/shard_map/all_gather | solution.py:120
  8.7 64.9 %copy-start.10 = (bf16[1,256,1024]{2,1,0:T(8,128)(2,1)S(1)}, bf16[1,256,1024]{2,1,0:T(8,128)(2,1)}, u32[]{:S(2)}) copy-start(bf16[1,256,1024]{2,1,0:T(8,128)(2,1)} %param.11) | copy-start | bytes 1572868
  8.7 266.4 %all-gather.11.cloned.1.call-start = ((), (), s32[]{:S(2)}) async-start(), calls=%async_computation.15 | async-start | bytes 35651584 | tf_op jit(solution)/shard_map/all_gather | solution.py:213
  12.9 391.1 %all-gather.13.cloned.1.call-start = ((), (), s32[]{:S(2)}) async-start(), calls=%async_computation.16 | async-start | bytes 17825792 | tf_op jit(solution)/shard_map/all_gather | solution.py:214
  81.6 19.5 %all-to-all-start = ((bf16[256,2,256]{2,0,1:T(8,128)(2,1)}), bf16[256,2,256]{2,0,1:T(8,128)(2,1)}, u32[]{:S(2)}, u32[]{:S(2)}) async-start(bf16[256,2,256]{2,0,1:T(8,128)(2,1)} %bitcast.262), calls=%async_computation | async-start | bytes 524288 | tf_op jit(solution)/shard_map/all_to_all | solution.py:155
  101.1 9.4 all-to-all-start.1
  110.5 10.3 all-to-all-start.2
  114.3 36.8 %copy-start.8 = (f32[256,1024]{1,0:T(8,128)}, f32[256,1024]{1,0:T(8,128)S(1)}, u32[]{:S(2)}) copy-start(f32[256,1024]{1,0:T(8,128)S(1)} %bitcast_convert_fusion) | copy-start | bytes 3145732
  129.0 34.8 %all-to-all-start.3 = ((bf16[2,256,512]{1,2,0:T(8,128)(2,1)}), bf16[2,256,512]{1,2,0:T(8,128)(2,1)S(1)}, u32[]{:S(2)}, u32[]{:S(2)}) async-start(bf16[2,256,512]{1,2,0:T(8,128)(2,1)} %copy.143), calls=%async_computation.3 | async-start | bytes 1048576 | tf_op jit(solution)/shard_map/all_to_all | solution.py:191
  132.5 607.9 %reduce-scatter.10.cloned.1.call-start = ((), (), s32[]{:S(2)}) async-start(), calls=%async_computation.18 | async-start | bytes 4456448 | tf_op jit(solution)/shard_map/reduce_scatter | solution.py:319
  522.9 12.2 all-to-all-start.4
  550.5 11.1 all-to-all-start.6
  561.6 11.4 all-to-all-start.5
  573.0 8.6 all-to-all-start.7
  576.4 165.6 %reduce-scatter.8.cloned.1.call-start = ((), (), s32[]{:S(2)}) async-start(), calls=%async_computation.17 | async-start | bytes 8912896 | tf_op jit(solution)/shard_map/reduce_scatter | solution.py:318
  586.3 445.4 %reduce-scatter.14.cloned.1.call-start = ((), (), s32[]{:S(2)}) async-start(), calls=%async_computation.20 | async-start | bytes 35651584 | tf_op jit(solution)/shard_map/reduce_scatter | solution.py:323
  640.5 1026.9 %reduce-scatter.12.cloned.1.call-start = ((), (), s32[]{:S(2)}) async-start(), calls=%async_computation.19 | async-start | bytes 71303168 | tf_op jit(solution)/shard_map/reduce_scatter | solution.py:322
  737.7 989.2 %reduce-scatter.16.cloned.1.call-start = ((), (), s32[]{:S(2)}) async-start(), calls=%async_computation.21 | async-start | bytes 557056
  740.3 1083.8 %all-reduce.12.cloned.1.call-start = ((), (), s32[]{:S(2)}) async-start(), calls=%async_computation.22 | async-start | bytes 7077888 | tf_op jit(solution)/shard_map/psum | solution.py:327
  1671.3 61.0 %copy-start.48 = (f32[1024]{0:T(1024)S(1)}, f32[1024]{0:T(1024)}, u32[]{:S(2)}) copy-start(f32[1024]{0:T(1024)} %get-tuple-element.32) | copy-start | bytes 12292
  1671.3 98.6 %copy-start.7 = (f32[256,1024]{1,0:T(8,128)S(1)}, f32[256,1024]{1,0:T(8,128)}, u32[]{:S(2)}) copy-start(f32[256,1024]{1,0:T(8,128)} %copy-done.6) | copy-start | bytes 3145732
  1671.3 98.6 %copy-start.55 = (f32[256]{0:T(256)S(1)}, f32[256]{0:T(256)}, u32[]{:S(2)}) copy-start(f32[256]{0:T(256)} %get-tuple-element.69) | copy-start | bytes 3076
  (56 other events, 545.4 us)
Sparse Core Ops, SparseCore 0:
  10.2 53.3 all-gather.6
  65.8 40.0 all-gather.8
  108.1 167.0 all-gather.10
  277.2 126.7 all-gather.12
  519.8 70.9 reduce-scatter.9
  594.7 102.4 reduce-scatter.7
  701.4 330.1 reduce-scatter.13
  1035.9 631.5 reduce-scatter.11
  1671.6 55.2 reduce-scatter.15
  1730.4 93.6 all-reduce.11
where the time goes:
time: 1850 us; the launch traced here: 1840 us
  waiting for transfers between devices  1240 us (67%)
  local copies, waits for them, and re-layouts  227 us (12%)
  matrix products  172 us (9%)
  blocking collectives  93.7 us (5%)
  other arithmetic  65.2 us (4%)
  starting transfers between devices  29.7 us (2%)
    reduce_scatter x1, waiting for transfers between devices, body(): lax.psum_scatter(gate_up_wgrad, 'dp', scatter_dimension=0, tiled=True)  633 us
    reduce_scatter x1, waiting for transfers between devices, body(): lax.psum_scatter(down_wgrad, 'dp', scatter_dimension=0, tiled=True)  288 us
    all_gather x1, waiting for transfers between devices, body(): lax.all_gather(w_down, 'dp', axis=0, tiled=True)  106 us
    all_gather x1, waiting for transfers between devices, body(): lax.all_gather(w_gate_up, 'dp', axis=0, tiled=True)  75.6 us
    transpose x1, local copies, waits for them, and re-layouts, body(): jnp.einsum('ecd,ecf->def', dispatched, gate_up_grad, preferred_element_ty...  68 us
    unnamed x2, blocking collectives  65.9 us
    unnamed x11, waiting for transfers between devices  55 us
    psum x1, waiting for transfers between devices, body(): lax.psum(shard_qkv.astype(jnp.bfloat16), 'seq').astype(jnp.float32)  51.8 us
  transfers between devices with their start and end apart: 18, of which 11 were waited for; matrix products, arithmetic and copies ran while one was open for 18% of the time, Pallas kernels for 0%

commit v1 on v0

--- a/solution.py
+++ b/solution.py
@@ -1,7 +1,9 @@
+import functools
 import jax
 import jax.numpy as jnp
 from jax import lax
 from jax.sharding import PartitionSpec as P
+from jax.lax import axis_index, axis_size, ppermute
 
 MODEL_WIDTH = 1024
 QUERY_HEADS = 16
@@ -15,6 +17,28 @@
 rope_base = 10000.0
 highest = lax.Precision.HIGHEST
 masked_score = -1e30
+
+
+def press_sites(local_x, k_dim):
+    local_x = jnp.moveaxis(local_x, 0, k_dim)
+    reached = local_x.shape
+    return local_x.reshape(
+        *reached[:k_dim], reached[k_dim] * reached[k_dim + 1], *reached[k_dim + 2 :]
+    )
+
+
+def resolve_words_here(base_x, which_dim, mesh_dim):
+    wide_n = axis_size(mesh_dim)
+    items = [base_x]
+    queue = tuple(((hop_no, (hop_no + 1) % wide_n) for hop_no in range(wide_n)))
+    while len(items) < wide_n:
+        items.append(ppermute(items[-1], mesh_dim, queue))
+    state_next = axis_index(mesh_dim)
+    items = jnp.stack(items)[(state_next - jnp.arange(wide_n)) % wide_n]
+    return press_sites(items, which_dim)
+
+
+_keep_up_levels_all = functools.partial(resolve_words_here, which_dim=0, mesh_dim="dp")
 
 
 def rms_normed(token_rows, gain_row):
@@ -211,7 +235,7 @@
     )
     full_gate_up, full_down = (
         lax.all_gather(w_gate_up, "dp", axis=0, tiled=True),
-        lax.all_gather(w_down, "dp", axis=0, tiled=True),
+        _keep_up_levels_all(w_down),
     )
     gate_up = jnp.einsum(
         "ecd,def->ecf", dispatched, full_gate_up, preferred_element_type=jnp.float32

time: 1850 us -> 1970 us (1.065)
  local copies, waits for them, and re-layouts: 227 us -> 266 us
  blocking collectives: 93.7 us -> 120 us
  matrix products: 172 us -> 192 us
  waiting for transfers between devices: 1240 us -> 1260 us
    ppermute x0 -> x15, waiting for transfers between devices: none -> 213 us  [resolve_words_here(): items.append(ppermute(items[-1], mesh_dim, queue))]
    all_gather x1 -> x0, waiting for transfers between devices: 106 us -> none  [body(): lax.all_gather(w_down, 'dp', axis=0, tiled=True)]
    all_gather x1, waiting for transfers between devices: 75.6 us -> 0.01 us  [body(): lax.all_gather(w_gate_up, 'dp', axis=0, tiled=True)]
    unnamed x136 -> x152, local copies, waits for them, and re-layouts: 14 us -> 45.8 us
    unnamed x2, blocking collectives: 65.9 us -> 91.3 us
    unnamed x11 -> x10, waiting for transfers between devices: 55 us -> 55 us
  transfers between devices with their start and end apart: 18 -> 32, of which waited for: 11 -> 21; matrix products, arithmetic and copies ran while one was open for 18% -> 18% of each run, Pallas kernels for 0% -> 0%
where the time goes in v1:
time: 1970 us; the launch traced here: 1950 us
  waiting for transfers between devices  1260 us (64%)
  local copies, waits for them, and re-layouts  266 us (14%)
  matrix products  192 us (10%)
  blocking collectives  120 us (6%)
  other arithmetic  64.4 us (3%)
  starting transfers between devices  31.6 us (2%)
    reduce_scatter x1, waiting for transfers between devices, body(): lax.psum_scatter(gate_up_wgrad, 'dp', scatter_dimension=0, tiled=True)  633 us
    reduce_scatter x1, waiting for transfers between devices, body(): lax.psum_scatter(down_wgrad, 'dp', scatter_dimension=0, tiled=True)  290 us
    ppermute x15, waiting for transfers between devices, resolve_words_here(): items.append(ppermute(items[-1], mesh_dim, queue))  213 us
    unnamed x2, blocking collectives  91.3 us
    transpose x1, local copies, waits for them, and re-layouts, body(): jnp.einsum('ecd,ecf->def', dispatched, gate_up_grad, preferred_element_ty...  68.3 us
    unnamed x10, waiting for transfers between devices  55 us
    psum x1, waiting for transfers between devices, body(): lax.psum(shard_qkv.astype(jnp.bfloat16), 'seq').astype(jnp.float32)  52.1 us
    unnamed x152, local copies, waits for them, and re-layouts  45.8 us
  transfers between devices with their start and end apart: 32, of which 21 were waited for; matrix products, arithmetic and copies ran while one was open for 18% of the time, Pallas kernels for 0%

profile of v1, /device:TPU:0, one launch (start us, length us, event | category | flops | bytes accessed | tf_op | source)
XLA Modules:
  0.0 1953.2 jit_solution(6280340109610934071)
XLA Ops:
  13.4 26.1 %collective-permute-done = bf16[32,16,1024]{2,1,0:T(8,128)(2,1)S(1)} collective-permute-done((bf16[32,16,1024]{2,1,0:T(8,128)(2,1)}, bf16[32,16,1024]{2,1,0:T(8,128)(2,1)S(1)}, u32[]{:S(2)}, u32[]{:S(2)}) %collective-permute-start) | collective-permute-done | bytes 1048608 | tf_op jit(solution)/shard_map/ppermute | solution.py:35
  39.5 33.5 %collective-permute-done.1 = bf16[32,16,1024]{2,1,0:T(8,128)(2,1)S(1)} collective-permute-done((bf16[32,16,1024]{2,1,0:T(8,128)(2,1)S(1)}, bf16[32,16,1024]{2,1,0:T(8,128)(2,1)S(1)}, u32[]{:S(2)}, u32[]{:S(2)}) %collective-permute-start.1) | collective-permute-done | bytes 1048608 | tf_op jit(solution)/shard_map/ppermute | solution.py:35
  93.0 22.2 %collective-permute-done.3 = bf16[32,16,1024]{2,1,0:T(8,128)(2,1)} collective-permute-done((bf16[32,16,1024]{2,1,0:T(8,128)(2,1)}, bf16[32,16,1024]{2,1,0:T(8,128)(2,1)}, u32[]{:S(2)}, u32[]{:S(2)}) %collective-permute-start.3) | collective-permute-done | bytes 1048608 | tf_op jit(solution)/shard_map/ppermute | solution.py:35
  133.3 39.0 %collective-permute-done.5 = bf16[32,16,1024]{2,1,0:T(8,128)(2,1)} collective-permute-done((bf16[32,16,1024]{2,1,0:T(8,128)(2,1)}, bf16[32,16,1024]{2,1,0:T(8,128)(2,1)}, u32[]{:S(2)}, u32[]{:S(2)}) %collective-permute-start.5) | collective-permute-done | bytes 1048608 | tf_op jit(solution)/shard_map/ppermute | solution.py:35
  174.0 61.4 %all-reduce.7 = (bf16[1024]{0:T(1024)(128)(2,1)S(1)}, bf16[1024]{0:T(1024)(128)(2,1)S(1)}) all-reduce(bf16[1024]{0:T(1024)(128)(2,1)S(1)} %dynamic-update-slice, bf16[1024]{0:T(1024)(128)(2,1)S(1)} %dynamic-update-slice.1), channel_id=1, replica_groups=mesh['seq'=2,'dp'=16] {'dp'}, use_global_device_ids=true, to_apply=%add.2 | all-reduce | flops 2048 | bytes 8192
  235.4 18.4 all-gather.1
  282.5 30.2 %collective-permute-done.7 = bf16[32,16,1024]{2,1,0:T(8,128)(2,1)} collective-permute-done((bf16[32,16,1024]{2,1,0:T(8,128)(2,1)}, bf16[32,16,1024]{2,1,0:T(8,128)(2,1)}, u32[]{:S(2)}, u32[]{:S(2)}) %collective-permute-start.7) | collective-permute-done | bytes 1048608 | tf_op jit(solution)/shard_map/ppermute | solution.py:35
  393.3 13.2 collective-permute-done.12
  407.2 18.8 gather_fusion.3
  473.9 21.7 %fusion.86 = f32[16,224,1024]{2,1,0:T(8,128)} fusion(bf16[16,224,1024]{2,1,0:T(8,128)(2,1)} %bitcast.276, bf16[1024,16,1024]{2,0,1:T(8,128)(2,1)} %all-gather.10.cloned.1.call-done), kind=kOutput, calls=%fused_computation.211 | convolution fusion | flops 7516192768 | bytes 55574528 | tf_op jit(solution)/shard_map/ecd,def->ecf/dot_general | solution.py:240
  495.6 27.4 %multiply_convert_fusion.2 = (bf16[16,224,512]{2,1,0:T(8,128)(2,1)}, bf16[16,224,512]{2,1,0:T(8,128)(2,1)}, bf16[16,224,512]{2,1,0:T(8,128)(2,1)}) fusion(f32[16,224,1024]{2,1,0:T(8,128)} %fusion.86, bf16[512,16,1024]{2,1,0:T(8,128)(2,1)} %bitcast.278, f32[16,224,1024]{2,1,0:T(8,128)} %bitcast.274, f32[16,224]{1,0:T(8,128)S(1)} %mul.376), kind=kOutput, calls=%fused_computation.31 | convolution fusion | flops 3792961536 | bytes 57161728 | tf_op jit(solution)/shard_map/ecd,fed->ecf/dot_general | solution.py:245
  523.1 31.7 %fusion.2 = f32[16,224,1024]{2,1,0:T(8,128)} fusion(bf16[16,224,512]{2,1,0:T(8,128)(2,1)} %get-tuple-element.51, bf16[512,16,1024]{2,1,0:T(8,128)(2,1)} %bitcast.279), kind=kOutput, calls=%fused_computation.10 | convolution fusion | flops 3758096384 | bytes 35127296 | tf_op jit(solution)/shard_map/ecf,fed->ecd/dot_general | solution.py:244
  554.8 21.6 %fusion.12 = f32[16,224,1024]{2,1,0:T(8,128)} fusion(bf16[1024,16,1024]{2,0,1:T(8,128)(2,1)} %all-gather.10.cloned.1.call-done, bf16[16,224,512]{2,1,0:T(8,128)(2,1)} %get-tuple-element.50, bf16[16,224,512]{2,1,0:T(8,128)(2,1)} %get-tuple-element.49), kind=kOutput, calls=%fused_computation.36 | convolution fusion | flops 7530872832 | bytes 55574528 | tf_op jit(solution)/shard_map/ecf,def->ecd/dot_general | solution.py:255
  576.4 17.1 gather_fusion.5
  599.9 17.1 gather_fusion.2
  696.0 19.4 convolution_bitcast_fusion.1
  715.4 33.9 %copy.168 = f32[512,16,1024]{2,1,0:T(8,128)} copy(f32[512,16,1024]{0,2,1:T(8,128)} %convolution_bitcast_fusion.1) | data formatting | bytes 67108864 | tf_op jit(solution)/shard_map/ecf,ecd->fed/transpose | solution.py:248
  749.4 28.9 %convolution_bitcast_fusion = f32[1024,16,1024]{0,2,1:T(8,128)} fusion(bf16[16,224,1024]{2,1,0:T(8,128)(2,1)} %bitcast.277, bf16[16,224,512]{2,1,0:T(8,128)(2,1)} %get-tuple-element.50, bf16[16,224,512]{2,1,0:T(8,128)(2,1)} %get-tuple-element.49), kind=kOutput, calls=%fused_computation.7 | convolution fusion | flops 7530872832 | bytes 81788928 | tf_op jit(solution)/shard_map/ecd,ecf->def/dot_general | solution.py:252
  778.3 68.3 %copy.167 = f32[1024,16,1024]{2,1,0:T(8,128)} copy(f32[1024,16,1024]{0,2,1:T(8,128)} %convolution_bitcast_fusion) | data formatting | bytes 134217728 | tf_op jit(solution)/shard_map/ecd,ecf->def/transpose | solution.py:252
  853.2 290.2 %reduce-scatter.14.cloned.1.call-done = f32[32,16,1024]{2,1,0:T(8,128)} async-done(((f32[512,16,1024]{2,1,0:T(8,128)}), f32[32,16,1024]{2,1,0:T(8,128)}) %reduce-scatter.14.cloned.1.call-update) | async-done | bytes 2097168 | tf_op jit(solution)/shard_map/reduce_scatter | solution.py:347
  1146.1 633.0 %reduce-scatter.12.cloned.1.call-done = f32[64,16,1024]{2,1,0:T(8,128)} async-done(((f32[1024,16,1024]{2,1,0:T(8,128)}), f32[64,16,1024]{2,1,0:T(8,128)}) %reduce-scatter.12.cloned.1.call-update) | async-done | bytes 4194320 | tf_op jit(solution)/shard_map/reduce_scatter | solution.py:346
  1785.1 53.5 %reduce-scatter.16.cloned.1.call-done = f32[64,16]{1,0:T(8,128)} async-done(((f32[1024,16]{1,0:T(8,128)}), f32[64,16]{1,0:T(8,128)}) %reduce-scatter.16.cloned.1.call-update) | async-done | bytes 4112
  1843.9 30.0 %all-reduce.6 = (bf16[1024]{0:T(1024)(128)(2,1)S(1)}, bf16[1024]{0:T(1024)(128)(2,1)S(1)}) all-reduce(f32[1024]{0:T(1024)S(1)} %get-tuple-element.34, f32[1024]{0:T(1024)S(1)} %copy-done.50), channel_id=3, replica_groups=mesh['seq'=2,'dp'=16] {'dp'}, use_global_device_ids=true, to_apply=%region_24.25.clone | all-reduce | flops 2048 | bytes 12288
  1883.8 52.1 %all-reduce.12.cloned.1.call-done = (bf16[64,2048]{1,0:T(8,128)(2,1)}, bf16[64,1024]{1,0:T(8,128)(2,1)}, bf16[64,16,1024]{2,1,0:T(8,128)(2,1)}, bf16[32,16,1024]{2,1,0:T(8,128)(2,1)}) async-done(((bf16[64,2048]{1,0:T(8,128)(2,1)}, bf16[64,1024]{1,0:T(8,128)(2,1)}, bf16[64,16,1024]{2,1,0:T(8,128)(2,1)}, bf16[32,16,1024]{2,1,0:T(8,128)(2,1)}), (bf16[64,2048]{1,0:T(8,128)(2,1)}, bf16[64,1024]{1,0:T(8,128)(2,1)}, ...) | async-done | bytes 3538960 | tf_op jit(solution)/shard_map/psum | solution.py:351
  (366 shorter events, 327.6 us)
Async XLA Ops:
  7.2 307.7 %all-gather.6.cloned.1.call-start = ((), (), s32[]{:S(2)}) async-start(), calls=%async_computation.13 | async-start | bytes 4456448 | tf_op jit(solution)/shard_map/all_gather | solution.py:143
  8.0 381.3 %all-gather.8.cloned.1.call-start = ((), (), s32[]{:S(2)}) async-start(), calls=%async_computation.14 | async-start | bytes 2228224 | tf_op jit(solution)/shard_map/all_gather | solution.py:144
  8.7 465.2 %all-gather.10.cloned.1.call-start = ((), (), s32[]{:S(2)}) async-start(), calls=%async_computation.15 | async-start | bytes 35651584 | tf_op jit(solution)/shard_map/all_gather | solution.py:237
  12.9 26.6 %collective-permute-start = (bf16[32,16,1024]{2,1,0:T(8,128)(2,1)}, bf16[32,16,1024]{2,1,0:T(8,128)(2,1)S(1)}, u32[]{:S(2)}, u32[]{:S(2)}) collective-permute-start(bf16[32,16,1024]{2,1,0:T(8,128)(2,1)} %param.20), channel_id=1, source_target_pairs={{0,1},{1,2},{2,3},{3,4},{4,5},{5,6},{6,7},{7,8},{8,9},{9,10},{10,1... | collective-permute-start | bytes 3145736 | tf_op jit(solution)/shard_map/ppermute | solution.py:35
  39.5 33.5 %collective-permute-start.1 = (bf16[32,16,1024]{2,1,0:T(8,128)(2,1)S(1)}, bf16[32,16,1024]{2,1,0:T(8,128)(2,1)S(1)}, u32[]{:S(2)}, u32[]{:S(2)}) collective-permute-start(bf16[32,16,1024]{2,1,0:T(8,128)(2,1)S(1)} %collective-permute-done), channel_id=1, source_target_pairs={{0,1},{1,2},{2,3},{3,4},{4,5},{5,6},{6,7},{7,8},{8,9},{9,10},{10,1... | collective-permute-start | bytes 3145736 | tf_op jit(solution)/shard_map/ppermute | solution.py:35
  73.0 19.6 %collective-permute-start.2 = (bf16[32,16,1024]{2,1,0:T(8,128)(2,1)S(1)}, bf16[32,16,1024]{2,1,0:T(8,128)(2,1)}, u32[]{:S(2)}, u32[]{:S(2)}) collective-permute-start(bf16[32,16,1024]{2,1,0:T(8,128)(2,1)S(1)} %collective-permute-done.1), channel_id=1, source_target_pairs={{0,1},{1,2},{2,3},{3,4},{4,5},{5,6},{6,7},{7,8},{8,9},{9,10},{10,1... | collective-permute-start | bytes 3145736 | tf_op jit(solution)/shard_map/ppermute | solution.py:35
  92.6 22.5 %collective-permute-start.3 = (bf16[32,16,1024]{2,1,0:T(8,128)(2,1)}, bf16[32,16,1024]{2,1,0:T(8,128)(2,1)}, u32[]{:S(2)}, u32[]{:S(2)}) collective-permute-start(bf16[32,16,1024]{2,1,0:T(8,128)(2,1)} %collective-permute-done.2), channel_id=1, source_target_pairs={{0,1},{1,2},{2,3},{3,4},{4,5},{5,6},{6,7},{7,8},{8,9},{9,10},{10,1... | collective-permute-start | bytes 3145736 | tf_op jit(solution)/shard_map/ppermute | solution.py:35
  115.1 17.3 collective-permute-start.4
  132.4 39.8 %collective-permute-start.5 = (bf16[32,16,1024]{2,1,0:T(8,128)(2,1)}, bf16[32,16,1024]{2,1,0:T(8,128)(2,1)}, u32[]{:S(2)}, u32[]{:S(2)}) collective-permute-start(bf16[32,16,1024]{2,1,0:T(8,128)(2,1)} %collective-permute-done.4), channel_id=1, source_target_pairs={{0,1},{1,2},{2,3},{3,4},{4,5},{5,6},{6,7},{7,8},{8,9},{9,10},{10,1... | collective-permute-start | bytes 3145736 | tf_op jit(solution)/shard_map/ppermute | solution.py:35
  172.3 100.5 %collective-permute-start.6 = (bf16[32,16,1024]{2,1,0:T(8,128)(2,1)}, bf16[32,16,1024]{2,1,0:T(8,128)(2,1)}, u32[]{:S(2)}, u32[]{:S(2)}) collective-permute-start(bf16[32,16,1024]{2,1,0:T(8,128)(2,1)} %collective-permute-done.5), channel_id=1, source_target_pairs={{0,1},{1,2},{2,3},{3,4},{4,5},{5,6},{6,7},{7,8},{8,9},{9,10},{10,1... | collective-permute-start | bytes 3145736 | tf_op jit(solution)/shard_map/ppermute | solution.py:35
  272.8 39.8 %collective-permute-start.7 = (bf16[32,16,1024]{2,1,0:T(8,128)(2,1)}, bf16[32,16,1024]{2,1,0:T(8,128)(2,1)}, u32[]{:S(2)}, u32[]{:S(2)}) collective-permute-start(bf16[32,16,1024]{2,1,0:T(8,128)(2,1)} %collective-permute-done.6), channel_id=1, source_target_pairs={{0,1},{1,2},{2,3},{3,4},{4,5},{5,6},{6,7},{7,8},{8,9},{9,10},{10,1... | collective-permute-start | bytes 3145736 | tf_op jit(solution)/shard_map/ppermute | solution.py:35
  312.6 25.0 %collective-permute-start.8 = (bf16[32,16,1024]{2,1,0:T(8,128)(2,1)}, bf16[32,16,1024]{2,1,0:T(8,128)(2,1)}, u32[]{:S(2)}, u32[]{:S(2)}) collective-permute-start(bf16[32,16,1024]{2,1,0:T(8,128)(2,1)} %collective-permute-done.7), channel_id=1, source_target_pairs={{0,1},{1,2},{2,3},{3,4},{4,5},{5,6},{6,7},{7,8},{8,9},{9,10},{10,1... | collective-permute-start | bytes 3145736 | tf_op jit(solution)/shard_map/ppermute | solution.py:35
  320.5 24.4 %all-to-all-start = ((bf16[256,2,256]{2,0,1:T(8,128)(2,1)}), bf16[256,2,256]{2,0,1:T(8,128)(2,1)}, u32[]{:S(2)}, u32[]{:S(2)}) async-start(bf16[256,2,256]{2,0,1:T(8,128)(2,1)} %bitcast.266), calls=%async_computation | async-start | bytes 524288 | tf_op jit(solution)/shard_map/all_to_all | solution.py:179
  337.6 17.2 collective-permute-start.9
  354.8 17.2 collective-permute-start.10
  372.1 17.2 collective-permute-start.11
  378.2 471.4 %reduce-scatter.10.cloned.1.call-start = ((), (), s32[]{:S(2)}) async-start(), calls=%async_computation.17 | async-start | bytes 4456448 | tf_op jit(solution)/shard_map/reduce_scatter | solution.py:343
  389.3 17.2 collective-permute-start.12
  406.5 36.2 %collective-permute-start.13 = (bf16[32,16,1024]{2,1,0:T(8,128)(2,1)}, bf16[32,16,1024]{2,1,0:T(8,128)(2,1)S(1)}, u32[]{:S(2)}, u32[]{:S(2)}) collective-permute-start(bf16[32,16,1024]{2,1,0:T(8,128)(2,1)} %collective-permute-done.12), channel_id=1, source_target_pairs={{0,1},{1,2},{2,3},{3,4},{4,5},{5,6},{6,7},{7,8},{8,9},{9,10},{10,1... | collective-permute-start | bytes 3145736 | tf_op jit(solution)/shard_map/ppermute | solution.py:35
  686.1 165.2 %reduce-scatter.8.cloned.1.call-start = ((), (), s32[]{:S(2)}) async-start(), calls=%async_computation.16 | async-start | bytes 8912896 | tf_op jit(solution)/shard_map/reduce_scatter | solution.py:342
  696.0 447.4 %reduce-scatter.14.cloned.1.call-start = ((), (), s32[]{:S(2)}) async-start(), calls=%async_computation.19 | async-start | bytes 35651584 | tf_op jit(solution)/shard_map/reduce_scatter | solution.py:347
  749.4 1029.7 %reduce-scatter.12.cloned.1.call-start = ((), (), s32[]{:S(2)}) async-start(), calls=%async_computation.18 | async-start | bytes 71303168 | tf_op jit(solution)/shard_map/reduce_scatter | solution.py:346
  846.7 991.9 %reduce-scatter.16.cloned.1.call-start = ((), (), s32[]{:S(2)}) async-start(), calls=%async_computation.20 | async-start | bytes 557056
  849.3 1086.6 %all-reduce.12.cloned.1.call-start = ((), (), s32[]{:S(2)}) async-start(), calls=%async_computation.21 | async-start | bytes 7077888 | tf_op jit(solution)/shard_map/psum | solution.py:351
  (72 other events, 2961.3 us)
Sparse Core Ops, SparseCore 0:
  10.2 61.4 all-gather.5
  73.9 47.2 all-gather.7
  123.4 205.9 all-gather.9
  632.6 70.0 reduce-scatter.9
  706.6 102.4 reduce-scatter.7
  813.2 330.1 reduce-scatter.13
  1147.6 631.4 reduce-scatter.11
  1783.2 55.2 reduce-scatter.15
  1842.2 93.6 all-reduce.11
